TPU v7x, 512 devices: a whole 4x4x16 slice. The times are simulated.
512 devices in a mesh: leaf: 16 (over z), front: 32 (over y, x, core).
Axes of the slice: x: 4, y: 4, z: 16, core: 2. Of those that a mesh axis runs over, the one named last changes fastest.
Arguments:
- stacked: float32 [32, 16384, 896], P('front', 'leaf'), may hold values from -1.171875 to 1.171875, as said below
- row_owner: int32 [32, 640, 1], P('front', 'leaf'), may hold values from 0 to 31; in each aligned block of 40 rows (0 to 39, 40 to 79, ..., all dimensions but the last counted through in order) at most 3 rows name the same one
- dest_local: int32 [32, 640], P('front', 'leaf'), may hold values from 0 to 63
Outputs:
- pivot_rows: float32 [32, 256, 896], P('front', 'leaf')
- assembled: float32 [32, 1024, 640], P('front', 'leaf')
Inputs may be any that keep to these rules, and one draw needn't show every extreme that they name: `stacked`: entries of a front's rows carry a scale of their row and one of their column. `row_owner`: among the 40 contribution rows of a front on one leaf index, no owner is named by more than 3 of them.
All inputs are finite; a program needn't handle non-finite values.
Results may differ from a plain program's by a relative error of at most 0.000076.
Values sent between devices are 32-bit elements; how exact they have to be, the bound alone decides.
No kernel may reach another device: no remote copies, remote signals or barrier semaphores. Data moves between devices by JAX's collectives and lax.ppermute only.
A program may use at most 64 MiB of HBM per device.

v0:
```python
import jax
import jax.numpy as jnp
from jax import lax
from jax.sharding import PartitionSpec as P

PIV = 256
PR_DEV = 64


highest = lax.Precision.HIGHEST


def shards(stacked, row_owner, dest_local):
    local_rows = stacked[0]
    gram_local = lax.dot_general(
        local_rows,
        local_rows,
        (((0,), (0,)), ((), ())),
        precision=highest,
        preferred_element_type=jnp.float32,
    )
    gram_total = lax.psum(gram_local, "leaf")
    upper_factor = jnp.linalg.cholesky(gram_total).T
    leaf_index = lax.axis_index("leaf")
    pivot_count = PIV // lax.axis_size("leaf")
    pivot_part = lax.dynamic_slice_in_dim(upper_factor, leaf_index * pivot_count, pivot_count, 0)
    contrib_count = row_owner.shape[1]
    block_rows = lax.dynamic_slice_in_dim(
        upper_factor, PIV + leaf_index * contrib_count, contrib_count, 0
    )[:, PIV:]
    owners = row_owner[0, :, 0]
    targets = dest_local[0]
    own_front = lax.axis_index("front").astype(jnp.float32)
    target_rows = lax.broadcasted_iota(jnp.float32, (PR_DEV, 1), 0)
    rows_piece = lax.all_gather(block_rows, "front", axis=0, tiled=True)
    owner_piece = lax.all_gather(owners.astype(jnp.float32), "front", axis=0, tiled=True)
    dest_piece = lax.all_gather(targets.astype(jnp.float32), "front", axis=0, tiled=True)
    hits = (dest_piece[None, :] == target_rows) & (owner_piece[None, :] == own_front)
    assembled = jnp.dot(
        hits.astype(jnp.float32), rows_piece, precision=highest, preferred_element_type=jnp.float32
    )
    return (pivot_part[None], assembled[None])


def solution(mesh):
    return jax.shard_map(
        shards,
        mesh=mesh,
        in_specs=(P("front", "leaf", None), P("front", "leaf", None), P("front", "leaf")),
        out_specs=(P("front", "leaf", None), P("front", "leaf", None)),
        check_vma=False,
    )
```

profile of v0, /device:TPU:1, one launch (start us, length us, event | category | flops | bytes accessed | tf_op | source)
XLA Modules:
  0.0 501.4 jit_solution(3690786755537206787)
XLA Ops:
  7.2 15.7 %fusion = f32[896,896]{0,1:T(8,128)} fusion(f32[1,1024,896]{2,1,0:T(8,128)} %param.3), kind=kOutput, calls=%fused_computation | convolution fusion | flops 9865003008 | bytes 6881280 | tf_op jit(solution)/shard_map/dot_general | solution.py:15
  23.0 147.0 %all-reduce.6.cloned.1.call-done = f32[896,896]{0,1:T(8,128)} async-done(((f32[896,896]{0,1:T(8,128)}), f32[896,896]{0,1:T(8,128)}) %all-reduce.6.cloned.1.call-update) | async-done | bytes 3211280 | tf_op jit(solution)/shard_map/psum | solution.py:22
  170.0 4.9 copy.15
  174.9 2.2 fusion.2
  177.2 1.7 copy-done.1
  178.8 11.7 %cholesky.195 = f32[128,128]{1,0:T(8,128)S(1)} custom-call(f32[128,128]{1,0:T(8,128)S(1)} %cholesky.502), custom_call_target="Cholesky" | custom-call | tf_op jit(solution)/shard_map/jit(cholesky)/cholesky | solution.py:23
  190.6 9.8 %custom-call.51 = f32[1,128,128]{1,2,0:T(8,128)S(1)} custom-call(f32[1,128,128]{2,1,0:T(8,128)S(1)} %get-tuple-element.26), custom_call_target="InvertDiagBlocksLowerTriangular" | custom-call | tf_op jit(solution)/shard_map/jit(cholesky)/cholesky | solution.py:23
  200.4 1.5 fusion.8
  201.9 0.9 copy.16
  202.8 1.8 convolution_subtract_fusion
  204.9 0.5 copy-done.3
  205.4 11.7 %cholesky.216 = f32[128,128]{1,0:T(8,128)S(1)} custom-call(f32[128,128]{1,0:T(8,128)S(1)} %cholesky.506), custom_call_target="Cholesky" | custom-call | tf_op jit(solution)/shard_map/jit(cholesky)/cholesky | solution.py:23
  217.1 1.0 constant_dynamic-update-slice_fusion.4
  218.2 9.9 %custom-call.52 = f32[1,128,128]{1,2,0:T(8,128)S(1)} custom-call(f32[1,128,128]{2,1,0:T(8,128)S(1)} %get-tuple-element.23), custom_call_target="InvertDiagBlocksLowerTriangular" | custom-call | tf_op jit(solution)/shard_map/jit(cholesky)/cholesky | solution.py:23
  228.1 1.4 convolution_dynamic-update-slice_fusion
  229.5 1.7 convolution_subtract_fusion.1
  231.1 0.6 cholesky.511
  231.8 13.2 %cholesky.411 = f32[128,128]{1,0:T(8,128)} custom-call(f32[128,128]{1,0:T(8,128)} %cholesky.511), custom_call_target="Cholesky" | custom-call | tf_op jit(solution)/shard_map/jit(cholesky)/cholesky | solution.py:23
  245.0 1.5 select_reduce_fusion.4
  246.4 0.6 compare_reduce_fusion.4
  247.1 11.3 %custom-call.53 = f32[1,128,128]{1,2,0:T(8,128)} custom-call(f32[1,128,128]{2,1,0:T(8,128)} %get-tuple-element.20), custom_call_target="InvertDiagBlocksLowerTriangular" | custom-call | tf_op jit(solution)/shard_map/jit(cholesky)/cholesky | solution.py:23
  258.3 1.2 convolution_dynamic-update-slice_fusion.1
  259.6 1.7 convolution_subtract_fusion.2
  261.3 12.7 %cholesky.430 = f32[128,128]{1,0:T(8,128)} custom-call(f32[128,128]{1,0:T(8,128)S(1)} %cholesky.516), custom_call_target="Cholesky" | custom-call | tf_op jit(solution)/shard_map/jit(cholesky)/cholesky | solution.py:23
  274.0 0.9 select_reduce_fusion.3
  274.9 0.6 compare_reduce_fusion.3
  275.5 10.4 %custom-call.54 = f32[1,128,128]{1,2,0:T(8,128)} custom-call(f32[1,128,128]{2,1,0:T(8,128)S(1)} %get-tuple-element.17), custom_call_target="InvertDiagBlocksLowerTriangular" | custom-call | tf_op jit(solution)/shard_map/jit(cholesky)/cholesky | solution.py:23
  286.0 1.1 convolution_dynamic-update-slice_fusion.2
  287.1 1.7 convolution_subtract_fusion.3
  288.9 11.7 %cholesky.449 = f32[128,128]{1,0:T(8,128)S(1)} custom-call(f32[128,128]{1,0:T(8,128)S(1)} %cholesky.521), custom_call_target="Cholesky" | custom-call | tf_op jit(solution)/shard_map/jit(cholesky)/cholesky | solution.py:23
  300.6 0.7 compare_reduce_fusion.2
  301.3 9.8 %custom-call.55 = f32[1,128,128]{1,2,0:T(8,128)S(1)} custom-call(f32[1,128,128]{2,1,0:T(8,128)S(1)} %get-tuple-element.14), custom_call_target="InvertDiagBlocksLowerTriangular" | custom-call | tf_op jit(solution)/shard_map/jit(cholesky)/cholesky | solution.py:23
  311.1 0.3 convolution_dynamic-update-slice_fusion.3
  311.4 1.8 convolution_subtract_fusion.4
  313.2 11.7 %cholesky.469 = f32[128,128]{1,0:T(8,128)S(1)} custom-call(f32[128,128]{1,0:T(8,128)S(1)} %cholesky.526), custom_call_target="Cholesky" | custom-call | tf_op jit(solution)/shard_map/jit(cholesky)/cholesky | solution.py:23
  324.9 0.7 compare_reduce_fusion.1
  325.6 9.8 %custom-call.56 = f32[1,128,128]{1,2,0:T(8,128)S(1)} custom-call(f32[1,128,128]{2,1,0:T(8,128)S(1)} %get-tuple-element.11), custom_call_target="InvertDiagBlocksLowerTriangular" | custom-call | tf_op jit(solution)/shard_map/jit(cholesky)/cholesky | solution.py:23
  335.7 1.3 convolution_subtract_fusion.5
  337.0 11.7 %cholesky.487 = f32[128,128]{1,0:T(8,128)S(1)} custom-call(f32[128,128]{1,0:T(8,128)S(1)} %convolution_subtract_fusion.5), custom_call_target="Cholesky" | custom-call | tf_op jit(solution)/shard_map/jit(cholesky)/cholesky | solution.py:23
  348.7 0.6 compare_reduce_fusion
  349.4 0.6 compare_reduce_fusion.5
  354.6 1.7 copy-done.2
  356.5 0.8 copy.22
  357.3 1.3 dynamic-slice.8
  359.5 129.0 %all-reduce.3 = (f32[1280]{0:T(1024)S(1)}, f32[1280]{0:T(1024)S(1)}) all-reduce(f32[1280]{0:T(1024)S(1)} %bitcast_dynamic-update-slice_fusion.1, f32[1280]{0:T(1024)S(1)} %bitcast_dynamic-update-slice_fusion), channel_id=2, replica_groups=mesh['leaf'=16,'front'=32] {'front'}, use_global_device_ids=true, to_apply=%add.1 | all-reduce | flops 2560 | bytes 20480
  488.5 1.2 dynamic-slice_bitcast_fusion.1
  489.7 0.8 copy.23
  490.5 3.9 convolution_bitcast_fusion
  (34 shorter events, 1.4 us)
Async XLA Ops:
  7.2 162.8 %all-reduce.6.cloned.1.call-start = ((), (), s32[]{:S(2)}) async-start(), calls=%async_computation | async-start | bytes 6422528 | tf_op jit(solution)/shard_map/psum | solution.py:22
  22.9 467.6 %all-gather.4.cloned.1.call-start = ((), (), s32[]{:S(2)}) async-start(), calls=%async_computation.1 | async-start | bytes 3379200 | tf_op jit(solution)/shard_map/all_gather | solution.py:35
  170.0 4.9 copy-start
  177.2 1.7 copy-start.1
  204.6 0.7 copy-start.3
  354.3 4.9 copy-start.4
  354.3 5.0 %copy-start.5 = (s32[1,40]{1,0:T(1,128)S(1)}, s32[1,40]{1,0:T(1,128)}, u32[]{:S(2)}) copy-start(s32[1,40]{1,0:T(1,128)} %param.5) | copy-start | bytes 484
  354.6 1.7 copy-start.2
Sparse Core Ops, SparseCore 0:
  23.0 146.9 all-reduce.5
  357.4 66.2 all-gather.3
where the time goes:
time: 510 us; the launch traced here: 501 us
  other arithmetic  155 us (30%)
  waiting for transfers between devices  147 us (29%)
  blocking collectives  129 us (25%)
  matrix products  35.2 us (7%)
  between operations  19.5 us (4%)
  local copies, waits for them, and re-layouts  15.9 us (3%)
    another operation x26, other arithmetic, shards(): upper_factor = jnp.linalg.cholesky(gram_total).T  152 us
    psum x1, waiting for transfers between devices, shards(): gram_total = lax.psum(gram_local, 'leaf')  147 us
    unnamed x1, blocking collectives  129 us
    another operation x12, matrix products, shards(): upper_factor = jnp.linalg.cholesky(gram_total).T  15.7 us
    dot_general x1, matrix products, shards(): lax.dot_general(local_rows, local_rows, (((0,), (0,)), ((), ())), precisi...  15.7 us
  transfers between devices with their start and end apart: 2, of which 1 were waited for; matrix products, arithmetic and copies ran while one was open for 1% of the time, Pallas kernels for 0%

commit v1 on v0

v1 whole, which is shorter than its diff:
```python
import functools
import jax
import jax.numpy as jnp
from jax import lax
from jax.experimental import pallas as pl
from jax.experimental.pallas import tpu as pltpu
from jax.sharding import PartitionSpec as P

PIV = 256
PR_DEV = 64
COLS = 896
CB = 640
CB_DEV = 40
CAP = 3
T = 128
NT = COLS // T
SUB = 8
NLEAF = 16
NFRONT = 32
PACKED = NT * (NT + 1) // 2 * T
SHARD = PACKED // NLEAF
PAD_SHARD = SHARD + 1
UNIT = 16
F32 = jnp.float32
BF16 = jnp.bfloat16
HIGHEST = lax.Precision.HIGHEST


def tile_index(i, j):
    return i * NT - i * (i - 1) // 2 + (j - i)


def halves(x):
    high = x.astype(BF16)
    return high, (x - high.astype(F32)).astype(BF16)


def dot_t(a, b):
    return lax.dot_general(a, b, (((0,), (0,)), ((), ())), preferred_element_type=F32)


def dot3_t(a, b):
    return dot_t(a[0], b[0]) + (dot_t(a[0], b[1]) + dot_t(a[1], b[0]))


def dot3(a, b):
    mm = functools.partial(jnp.dot, preferred_element_type=F32)
    return mm(a[0], b[0]) + (mm(a[0], b[1]) + mm(a[1], b[0]))


def gram_kernel(x_ref, out_ref, acc_ref):
    step = pl.program_id(0)

    @pl.when(step == 0)
    def _():
        acc_ref[...] = jnp.zeros_like(acc_ref)

    high, low = halves(x_ref[0])
    for start in range(0, COLS, 2 * T):
        stop = min(start + 2 * T, COLS)
        a = (high[:, :stop], low[:, :stop])
        b = (high[:, start:stop], low[:, start:stop])
        block = dot3_t(a, b)
        for j in range(start // T, stop // T):
            for i in range(j + 1):
                row = tile_index(i, j) * T
                acc_ref[row : row + T, :] += block[i * T : (i + 1) * T, j * T - start : (j + 1) * T - start]

    @pl.when(step == pl.num_programs(0) - 1)
    def _():
        for z in range(NLEAF):
            out_ref[z * PAD_SHARD : z * PAD_SHARD + SHARD, :] = acc_ref[z * SHARD : (z + 1) * SHARD, :]
            out_ref[z * PAD_SHARD + SHARD : (z + 1) * PAD_SHARD, :] = jnp.zeros((PAD_SHARD - SHARD, T), F32)


def local_gram(stacked):
    rows = stacked.shape[1]
    chunk = 256
    return pl.pallas_call(
        gram_kernel,
        out_shape=jax.ShapeDtypeStruct((NLEAF * PAD_SHARD, T), F32),
        grid=(rows // chunk,),
        in_specs=[pl.BlockSpec((1, chunk, COLS), lambda k: (0, k, 0))],
        out_specs=pl.BlockSpec((NLEAF * PAD_SHARD, T), lambda k: (0, 0)),
        scratch_shapes=[pltpu.VMEM((PACKED, T), F32)],
        name="local_gram",
    )(stacked)


def lanes_of(x, lane):
    return jnp.broadcast_to(x[:, lane : lane + 1], (SUB, T))


def row_of(x, row):
    return jnp.broadcast_to(x[row : row + 1, :], (SUB, T))


def diagonal_factor(d_ref, inv_ref):
    lane = lax.broadcasted_iota(jnp.int32, (SUB, T), 1)
    sub = lax.broadcasted_iota(jnp.int32, (SUB, T), 0)
    nb = T // SUB
    rows = [d_ref[SUB * i : SUB * (i + 1), :] for i in range(nb)]
    unit = [(lane == sub + SUB * i).astype(F32) for i in range(nb)]
    for b in range(nb):
        c0 = SUB * b
        columns = [lanes_of(rows[b], c0 + k) for k in range(SUB)]
        s = [[None] * SUB for _ in range(SUB)]
        for i in range(SUB):
            for k in range(i + 1):
                s[i][k] = s[k][i] = row_of(columns[k], i)
        r = [row_of(rows[b], k) for k in range(SUB)]
        e = [row_of(unit[b], k) for k in range(SUB)]
        for k in range(SUB):
            root = lax.rsqrt(s[k][k])
            inverse = root * root
            at = c0 + k
            u = jnp.where(lane >= c0 + k, r[k] * root, 0.0)
            d_ref[at : at + 1, :] = u[0:1, :]
            inv_ref[at : at + 1, :] = (e[k] * root)[0:1, :]
            t = [s[k][j] * inverse if j > k else None for j in range(SUB)]
            pr = r[k] * inverse
            pe = e[k] * inverse
            for i in range(SUB):
                if i == k:
                    continue
                f = s[i][k]
                for j in range(k + 1, SUB):
                    if i < k or j >= i:
                        s[i][j] = s[i][j] - f * t[j]
                        if i > k:
                            s[j][i] = s[i][j]
                r[i] = r[i] - f * pr
                e[i] = e[i] - f * pe
            for j in range(k + 1, SUB):
                s[k][j] = t[j]
            r[k] = pr
            e[k] = pe
        for i in range(b + 1, nb):
            columns = [lanes_of(rows[i], c0 + k) for k in range(SUB)]
            acc_r = columns[0] * r[0]
            acc_e = columns[0] * e[0]
            for k in range(1, SUB):
                acc_r = acc_r + columns[k] * r[k]
                acc_e = acc_e + columns[k] * e[k]
            rows[i] = rows[i] - acc_r
            unit[i] = unit[i] - acc_e


def update_after(p, s_ref, d_ref, inv_ref):
    base = p * T
    after = base + T
    s_ref[base:after, base:after] = d_ref[...]
    if after == COLS:
        return
    panel = dot3(halves(inv_ref[...]), halves(s_ref[base:after, after:]))
    s_ref[base:after, after:] = panel
    split = halves(panel)
    for i in range(p + 1, NT):
        lo = i * T - after
        left = tuple(v[:, lo : lo + T] for v in split)
        right = tuple(v[:, lo:] for v in split)
        block = s_ref[i * T : (i + 1) * T, i * T :] - dot3_t(left, right)
        s_ref[i * T : (i + 1) * T, i * T :] = block
        if i == p + 1:
            d_ref[...] = block[:, :T]


def factor_kernel(g1_ref, g2_ref, owner_row_ref, owner_ref, dest_ref, leaf_ref, piv_ref, pay_ref, s_ref, d_ref, inv_ref):
    half = SHARD // 2
    per = half // UNIT
    for i in range(NT):
        for j in range(NT):
            if j < i:
                s_ref[i * T : (i + 1) * T, j * T : (j + 1) * T] = jnp.zeros((T, T), F32)
                continue
            for u in range(T // UNIT):
                g = tile_index(i, j) * (T // UNIT) + u
                z, rest = divmod(g, 2 * per)
                src = g1_ref if rest < per else g2_ref
                row = (z * per + rest % per) * UNIT
                s_ref[i * T + u * UNIT : i * T + (u + 1) * UNIT, j * T : (j + 1) * T] = src[row : row + UNIT, :]
    d_ref[...] = s_ref[:T, :T]

    def panel_step(p, _):
        diagonal_factor(d_ref, inv_ref)
        for q in range(NT):
            pl.when(p == q)(functools.partial(update_after, q, s_ref, d_ref, inv_ref))
        return 0

    lax.fori_loop(0, NT, panel_step, 0)
    leaf = leaf_ref[0]
    piv_ref[0] = s_ref[pl.ds(pl.multiple_of(leaf * (PIV // NLEAF), 8), PIV // NLEAF), :]
    block = s_ref[pl.ds(pl.multiple_of(PIV + leaf * CB_DEV, 8), CB_DEV), PIV:]
    owner = owner_ref[...]
    same = owner == owner_row_ref[...]
    earlier = lax.broadcasted_iota(jnp.int32, (CB_DEV, CB_DEV), 1) < lax.broadcasted_iota(jnp.int32, (CB_DEV, CB_DEV), 0)
    slot = jnp.sum(jnp.where(same & earlier, 1.0, 0.0), axis=1, keepdims=True).astype(jnp.int32)
    place = slot * NFRONT + owner
    pick = (place == lax.broadcasted_iota(jnp.int32, (CB_DEV, CAP * NFRONT), 1)).astype(F32)
    marks = jnp.broadcast_to((dest_ref[...] + 1).astype(F32), (CB_DEV, T))
    send = lax.dot_general(
        pick, jnp.concatenate([block, marks], axis=1), (((0,), (0,)), ((), ())), precision=HIGHEST, preferred_element_type=F32
    )
    lane = lax.broadcasted_iota(jnp.int32, (NFRONT, T), 1)
    meta = jnp.zeros((NFRONT, T), F32)
    for k in range(CAP):
        part = send[k * NFRONT : (k + 1) * NFRONT, :]
        for t in range(CB // T):
            pay_ref[pl.ds(k * (CB // T) + t, NFRONT, stride=16), :] = part[:, t * T : (t + 1) * T]
        meta = jnp.where(lane == k, part[:, CB:], meta)
    pay_ref[pl.ds(15, NFRONT, stride=16), :] = meta


def factor(g1, g2, owner_row, owner, dest, leaf):
    vmem = pl.BlockSpec(memory_space=pltpu.VMEM)
    return pl.pallas_call(
        factor_kernel,
        out_shape=(
            jax.ShapeDtypeStruct((1, PIV // NLEAF, COLS), F32),
            jax.ShapeDtypeStruct((NFRONT * 16, T), F32),
        ),
        in_specs=[vmem] * 5 + [pl.BlockSpec(memory_space=pltpu.SMEM)],
        out_specs=(vmem, vmem),
        scratch_shapes=[pltpu.VMEM((COLS, COLS), F32), pltpu.VMEM((T, T), F32), pltpu.VMEM((T, T), F32)],
        name="factor",
    )(g1, g2, owner_row, owner, dest, leaf)


def assemble_kernel(pay_ref, out_ref):
    meta = pay_ref[pl.ds(15, NFRONT, stride=16), :]
    target = lax.broadcasted_iota(jnp.int32, (NFRONT, PR_DEV), 1).astype(F32) + 1.0
    total = jnp.zeros((PR_DEV, CB), F32)
    for k in range(CAP):
        hits = (meta[:, k : k + 1] == target).astype(F32)
        rows = jnp.concatenate(
            [pay_ref[pl.ds(k * (CB // T) + t, NFRONT, stride=16), :] for t in range(CB // T)], axis=1
        )
        total = total + lax.dot_general(
            hits, rows, (((0,), (0,)), ((), ())), precision=HIGHEST, preferred_element_type=F32
        )
    out_ref[0] = total


def assemble(pay):
    vmem = pl.BlockSpec(memory_space=pltpu.VMEM)
    return pl.pallas_call(
        assemble_kernel,
        out_shape=jax.ShapeDtypeStruct((1, PR_DEV, CB), F32),
        in_specs=[vmem],
        out_specs=vmem,
        name="assemble",
    )(pay)


def shards(stacked, row_owner, dest_local):
    gram = local_gram(stacked)
    piece = lax.optimization_barrier(lax.psum_scatter(gram, "leaf", scatter_dimension=0, tiled=True))
    half = SHARD // 2
    g1 = lax.all_gather(piece[:half], "leaf", axis=0, tiled=True)
    g2 = lax.all_gather(piece[half:SHARD], "leaf", axis=0, tiled=True)
    owner = row_owner[0]
    dest = dest_local.reshape(CB_DEV, 1)
    leaf = lax.axis_index("leaf").astype(jnp.int32).reshape(1)
    piv, pay = factor(g1, g2, owner.reshape(1, CB_DEV), owner, dest, leaf)
    got = lax.all_to_all(pay, "front", 0, 0, tiled=True)
    return piv, assemble(got)


def solution(mesh):
    return jax.shard_map(
        shards,
        mesh=mesh,
        in_specs=(P("front", "leaf", None), P("front", "leaf", None), P("front", "leaf")),
        out_specs=(P("front", "leaf", None), P("front", "leaf", None)),
        check_vma=False,
    )
```

time: 510 us -> 193 us (0.38); the launches traced: 501 us -> 193 us
  other arithmetic: 155 us -> 0 us
  waiting for transfers between devices: 147 us -> 0.01 us
  Pallas kernels: 0 us -> 49.6 us
  matrix products: 35.2 us -> 0 us
  between operations: 19.5 us -> 1.36 us
  local copies, waits for them, and re-layouts: 15.9 us -> 3.1 us
  blocking collectives: 129 us -> 136 us
    another operation x26 -> x0, other arithmetic: 152 us -> none  [shards(): upper_factor = jnp.linalg.cholesky(gram_total).T]
    psum x1 -> x0, waiting for transfers between devices: 147 us -> none  [shards(): gram_total = lax.psum(gram_local, 'leaf')]
    unnamed x1, blocking collectives: 129 us -> 41.5 us
    all_gather x0 -> x2, blocking collectives: none -> 58.4 us  [the longest x1 29.9 us: shards(): g2 = lax.all_gather(piece[half:SHARD], 'leaf', axis=0, tiled=True)]
    pallas_call x0 -> x3, Pallas kernels: none -> 49.6 us  [the longest x1 39.9 us: factor(): pl.pallas_call(factor_kernel, out_shape=(jax.ShapeDtypeStruct((1, PIV //...]
    all_to_all x0 -> x1, blocking collectives: none -> 35.7 us  [shards(): got = lax.all_to_all(pay, 'front', 0, 0, tiled=True)]
    dot_general x2 -> x0, matrix products: 19.5 us -> none  [the longest x1 15.7 us: shards(): lax.dot_general(local_rows, local_rows, (((0,), (0,)), ((), ())), precisi...]
    another operation x12 -> x0, matrix products: 15.7 us -> none  [shards(): upper_factor = jnp.linalg.cholesky(gram_total).T]
  transfers between devices with their start and end apart: 2 -> 1, of which waited for: 1 -> 0; matrix products, arithmetic and copies ran while one was open for 1% -> 1% of each run, Pallas kernels for 0% -> 0%
where the time goes in v1:
time: 193 us
  blocking collectives  136 us (70%)
  Pallas kernels  49.6 us (26%)
  local copies, waits for them, and re-layouts  3.1 us (2%)
  starting transfers between devices  2.98 us (2%)
    unnamed x1, blocking collectives  41.5 us
    pallas_call x1, Pallas kernels, factor(): pl.pallas_call(factor_kernel, out_shape=(jax.ShapeDtypeStruct((1, PIV //...  39.9 us
    all_to_all x1, blocking collectives, shards(): got = lax.all_to_all(pay, 'front', 0, 0, tiled=True)  35.7 us
    all_gather x1, blocking collectives, shards(): g2 = lax.all_gather(piece[half:SHARD], 'leaf', axis=0, tiled=True)  29.9 us
    all_gather x1, blocking collectives, shards(): g1 = lax.all_gather(piece[:half], 'leaf', axis=0, tiled=True)  28.5 us
    pallas_call x1, Pallas kernels, local_gram(): pl.pallas_call(gram_kernel, out_shape=jax.ShapeDtypeStruct((NLEAF * PAD_S...  7.44 us
  transfers between devices with their start and end apart: 1, of which 0 were waited for; matrix products, arithmetic and copies ran while one was open for 1% of the time, Pallas kernels for 0%

profile of v1, /device:TPU:1, one launch (start us, length us, event | category | flops | bytes accessed | tf_op | source)
XLA Modules:
  0.0 192.7 jit_solution(4907220283067021608)
XLA Ops:
  0.6 7.4 %local_gram.1 = f32[3600,128]{1,0:T(8,128)} custom-call(f32[1,1024,896]{2,1,0:T(8,128)} %x_ref.1), custom_call_target="tpu_custom_call" | custom-call | tf_op jit(solution)/shard_map/local_gram/pallas_call | solution.py:79
  8.1 0.0 copy-start.1
  8.1 0.0 copy-start
  8.1 41.5 %fusion = f32[240,128]{1,0:T(8,128)S(1)} fusion(f32[3600,128]{1,0:T(8,128)} %local_gram.1), kind=kCustom, calls=%all-reduce-scatter | all-reduce-scatter fusion | flops 491521 | bytes 1968128
  49.6 3.0 %collective-permute-start = (f32[225,128]{1,0:T(8,128)S(1)}, f32[225,128]{1,0:T(8,128)S(1)}, u32[]{:S(2)}, u32[]{:S(2)}) collective-permute-start(f32[225,128]{1,0:T(8,128)S(1)} %slice.10), channel_id=1, source_target_pairs={{0,32},{32,64},{64,96},{96,128},{128,160},{160,192},{192,224},{224... | collective-permute-start | bytes 345608
  52.6 0.0 copy-done.1
  52.6 0.7 copy.8.dest_ref
  53.3 0.0 copy-done
  53.3 0.7 copy.7.owner_ref
  54.0 1.3 dynamic-slice.4
  55.9 0.0 collective-permute-done
  55.9 0.4 concatenate
  56.4 29.9 %all_gather.7.g2_ref = f32[1792,128]{1,0:T(8,128)} all-gather(f32[112,128]{1,0:T(8,128)S(1)} %get-tuple-element.6), channel_id=1, replica_groups=mesh['leaf'=16,'front'=32] {'leaf'}, dimensions={0}, use_global_device_ids=true | all-gather | bytes 974848 | tf_op jit(solution)/shard_map/all_gather | solution.py:260
  86.3 28.5 %all_gather.6.g1_ref = f32[1792,128]{1,0:T(8,128)} all-gather(f32[112,128]{1,0:T(8,128)S(1)} %get-tuple-element.7), channel_id=1, replica_groups=mesh['leaf'=16,'front'=32] {'leaf'}, dimensions={0}, use_global_device_ids=true | all-gather | bytes 974848 | tf_op jit(solution)/shard_map/all_gather | solution.py:259
  114.8 39.9 %factor.1 = (f32[1,16,896]{2,1,0:T(8,128)}, f32[512,128]{1,0:T(8,128)}) custom-call(f32[1792,128]{1,0:T(8,128)} %all_gather.6.g1_ref, f32[1792,128]{1,0:T(8,128)} %all_gather.7.g2_ref, s32[1,40]{1,0:T(1,128)} %bitcast.11, s32[40,1]{1,0:T(8,128)} %copy.7.owner_ref, s32[40,1]{1,0:T(8,128)} %copy.8.dest_ref, s32[1]{0:T(128)} %bitcast.4.leaf_ref), custom_call_target="tpu_custom_call" | custom-call | tf_op jit(solution)/shard_map/factor/pallas_call | solution.py:216
  154.7 35.7 %all_to_all.11 = f32[32,16,128]{2,1,0:T(8,128)} all-to-all(f32[32,16,128]{2,1,0:T(8,128)} %bitcast.10), channel_id=1, replica_groups=mesh['leaf'=16,'front'=32] {'front'}, dimensions={0} | all-to-all | bytes 524288 | tf_op jit(solution)/shard_map/all_to_all | solution.py:265
  190.4 2.3 %assemble.1 = f32[1,64,640]{2,1,0:T(8,128)} custom-call(f32[512,128]{1,0:T(8,128)} %bitcast.9), custom_call_target="tpu_custom_call" | custom-call | tf_op jit(solution)/shard_map/assemble/pallas_call | solution.py:246
  (3 shorter events, 0.0 us)
Async XLA Ops:
  8.1 44.5 %copy-start.1 = (s32[1,40]{1,0:T(1,128)S(1)}, s32[1,40]{1,0:T(1,128)}, u32[]{:S(2)}) copy-start(s32[1,40]{1,0:T(1,128)} %param.5) | copy-start | bytes 484
  8.1 45.2 %copy-start = (s32[1,40,1]{1,2,0:T(1,128)S(1)}, s32[1,40,1]{1,2,0:T(1,128)}, u32[]{:S(2)}) copy-start(s32[1,40,1]{1,2,0:T(1,128)} %param.4) | copy-start | bytes 484
  49.6 6.3 %collective-permute-start = (f32[225,128]{1,0:T(8,128)S(1)}, f32[225,128]{1,0:T(8,128)S(1)}, u32[]{:S(2)}, u32[]{:S(2)}) collective-permute-start(f32[225,128]{1,0:T(8,128)S(1)} %slice.10), channel_id=1, source_target_pairs={{0,32},{32,64},{64,96},{96,128},{128,160},{160,192},{192,224},{224... | collective-permute-start | bytes 345608

commit v2 on v1

--- a/solution.py
+++ b/solution.py
@@ -84,11 +84,12 @@
         out_specs=pl.BlockSpec((NLEAF * PAD_SHARD, T), lambda k: (0, 0)),
         scratch_shapes=[pltpu.VMEM((PACKED, T), F32)],
         name="local_gram",
+        compiler_params=pltpu.CompilerParams(vmem_limit_bytes=61 << 20),
     )(stacked)
 
 
 def lanes_of(x, lane):
-    return jnp.broadcast_to(x[:, lane : lane + 1], (SUB, T))
+    return jnp.take_along_axis(x, jnp.full((SUB, T), lane, jnp.int32), axis=1)
 
 
 def row_of(x, row):
@@ -98,61 +99,45 @@
 def diagonal_factor(d_ref, inv_ref):
     lane = lax.broadcasted_iota(jnp.int32, (SUB, T), 1)
     sub = lax.broadcasted_iota(jnp.int32, (SUB, T), 0)
+    is_row = [sub == k for k in range(SUB)]
     nb = T // SUB
     rows = [d_ref[SUB * i : SUB * (i + 1), :] for i in range(nb)]
-    unit = [(lane == sub + SUB * i).astype(F32) for i in range(nb)]
     for b in range(nb):
         c0 = SUB * b
-        columns = [lanes_of(rows[b], c0 + k) for k in range(SUB)]
-        s = [[None] * SUB for _ in range(SUB)]
-        for i in range(SUB):
-            for k in range(i + 1):
-                s[i][k] = s[k][i] = row_of(columns[k], i)
-        r = [row_of(rows[b], k) for k in range(SUB)]
-        e = [row_of(unit[b], k) for k in range(SUB)]
+        inside = (lane >= c0) & (lane < c0 + SUB)
+        col = [lanes_of(rows[b], c0 + k) for k in range(SUB)]
+        work = jnp.where(inside, (lane == sub + c0).astype(F32), rows[b])
+        done = jnp.zeros((SUB, T), F32)
         for k in range(SUB):
-            root = lax.rsqrt(s[k][k])
+            root = lax.rsqrt(row_of(col[k], k))
             inverse = root * root
-            at = c0 + k
-            u = jnp.where(lane >= c0 + k, r[k] * root, 0.0)
-            d_ref[at : at + 1, :] = u[0:1, :]
-            inv_ref[at : at + 1, :] = (e[k] * root)[0:1, :]
-            t = [s[k][j] * inverse if j > k else None for j in range(SUB)]
-            pr = r[k] * inverse
-            pe = e[k] * inverse
-            for i in range(SUB):
-                if i == k:
-                    continue
-                f = s[i][k]
-                for j in range(k + 1, SUB):
-                    if i < k or j >= i:
-                        s[i][j] = s[i][j] - f * t[j]
-                        if i > k:
-                            s[j][i] = s[i][j]
-                r[i] = r[i] - f * pr
-                e[i] = e[i] - f * pe
+            ahead = [row_of(col[j], k) if j > k else None for j in range(SUB)]
             for j in range(k + 1, SUB):
-                s[k][j] = t[j]
-            r[k] = pr
-            e[k] = pe
+                prod = col[k] * ahead[j]
+                col[j] = jnp.where(is_row[k], ahead[j] * inverse, col[j] - prod * inverse)
+            rk = row_of(work, k)
+            done = jnp.where(is_row[k], rk * root, done)
+            pk = rk * inverse
+            work = jnp.where(is_row[k], pk, work - col[k] * pk)
+        inv_ref[c0 : c0 + SUB, :] = jnp.where(lane < c0 + SUB, done, 0.0)
+        if b + 1 < nb:
+            solved = [row_of(work, k) for k in range(SUB)]
         for i in range(b + 1, nb):
-            columns = [lanes_of(rows[i], c0 + k) for k in range(SUB)]
-            acc_r = columns[0] * r[0]
-            acc_e = columns[0] * e[0]
-            for k in range(1, SUB):
-                acc_r = acc_r + columns[k] * r[k]
-                acc_e = acc_e + columns[k] * e[k]
-            rows[i] = rows[i] - acc_r
-            unit[i] = unit[i] - acc_e
+            terms = [lanes_of(rows[i], c0 + k) * solved[k] for k in range(SUB)]
+            while len(terms) > 1:
+                terms = [terms[q] + terms[q + 1] for q in range(0, len(terms), 2)]
+            rows[i] = jnp.where(inside, 0.0, rows[i]) - terms[0]
 
 
 def update_after(p, s_ref, d_ref, inv_ref):
     base = p * T
     after = base + T
-    s_ref[base:after, base:after] = d_ref[...]
+    panel = dot3(halves(inv_ref[...]), halves(s_ref[base:after, base:]))
+    upper = lax.broadcasted_iota(jnp.int32, (T, T), 1) >= lax.broadcasted_iota(jnp.int32, (T, T), 0)
+    s_ref[base:after, base:after] = jnp.where(upper, panel[:, :T], 0.0)
     if after == COLS:
         return
-    panel = dot3(halves(inv_ref[...]), halves(s_ref[base:after, after:]))
+    panel = panel[:, T:]
     s_ref[base:after, after:] = panel
     split = halves(panel)
     for i in range(p + 1, NT):
@@ -165,20 +150,34 @@
             d_ref[...] = block[:, :T]
 
 
-def factor_kernel(g1_ref, g2_ref, owner_row_ref, owner_ref, dest_ref, leaf_ref, piv_ref, pay_ref, s_ref, d_ref, inv_ref):
-    half = SHARD // 2
-    per = half // UNIT
+def unpack(mine, parity, g_ref, low_ref, high_ref, s_ref):
+    per = SHARD // UNIT
     for i in range(NT):
-        for j in range(NT):
-            if j < i:
-                s_ref[i * T : (i + 1) * T, j * T : (j + 1) * T] = jnp.zeros((T, T), F32)
-                continue
+        for j in range(i, NT):
             for u in range(T // UNIT):
-                g = tile_index(i, j) * (T // UNIT) + u
-                z, rest = divmod(g, 2 * per)
-                src = g1_ref if rest < per else g2_ref
-                row = (z * per + rest % per) * UNIT
+                z, rest = divmod(tile_index(i, j) * (T // UNIT) + u, per)
+                if (z % 2 == parity) != mine:
+                    continue
+                row = (z // 2 * per + rest) * UNIT
+                src = g_ref
+                if not mine:
+                    half = NLEAF // 4 * SHARD
+                    src, row = (low_ref, row) if row < half else (high_ref, row - half)
                 s_ref[i * T + u * UNIT : i * T + (u + 1) * UNIT, j * T : (j + 1) * T] = src[row : row + UNIT, :]
+
+
+def factor_kernel(g_ref, low_ref, high_ref, owner_row_ref, owner_ref, dest_ref, leaf_ref, piv_ref, pay_ref, s_ref, d_ref, inv_ref):
+    for i in range(NT):
+        for j in range(i):
+            s_ref[i * T : (i + 1) * T, j * T : (j + 1) * T] = jnp.zeros((T, T), F32)
+    leaf = leaf_ref[0]
+    for parity in range(2):
+
+        @pl.when(lax.rem(leaf, 2) == parity)
+        def _():
+            for mine in (True, False):
+                unpack(mine, parity, g_ref, low_ref, high_ref, s_ref)
+
     d_ref[...] = s_ref[:T, :T]
 
     def panel_step(p, _):
@@ -188,7 +187,6 @@
         return 0
 
     lax.fori_loop(0, NT, panel_step, 0)
-    leaf = leaf_ref[0]
     piv_ref[0] = s_ref[pl.ds(pl.multiple_of(leaf * (PIV // NLEAF), 8), PIV // NLEAF), :]
     block = s_ref[pl.ds(pl.multiple_of(PIV + leaf * CB_DEV, 8), CB_DEV), PIV:]
     owner = owner_ref[...]
@@ -211,7 +209,7 @@
     pay_ref[pl.ds(15, NFRONT, stride=16), :] = meta
 
 
-def factor(g1, g2, owner_row, owner, dest, leaf):
+def factor(g, low, high, owner_row, owner, dest, leaf):
     vmem = pl.BlockSpec(memory_space=pltpu.VMEM)
     return pl.pallas_call(
         factor_kernel,
@@ -219,11 +217,12 @@
             jax.ShapeDtypeStruct((1, PIV // NLEAF, COLS), F32),
             jax.ShapeDtypeStruct((NFRONT * 16, T), F32),
         ),
-        in_specs=[vmem] * 5 + [pl.BlockSpec(memory_space=pltpu.SMEM)],
+        in_specs=[vmem] * 6 + [pl.BlockSpec(memory_space=pltpu.SMEM)],
         out_specs=(vmem, vmem),
         scratch_shapes=[pltpu.VMEM((COLS, COLS), F32), pltpu.VMEM((T, T), F32), pltpu.VMEM((T, T), F32)],
         name="factor",
-    )(g1, g2, owner_row, owner, dest, leaf)
+        compiler_params=pltpu.CompilerParams(vmem_limit_bytes=24 << 20),
+    )(g, low, high, owner_row, owner, dest, leaf)
 
 
 def assemble_kernel(pay_ref, out_ref):
@@ -249,19 +248,22 @@
         in_specs=[vmem],
         out_specs=vmem,
         name="assemble",
+        compiler_params=pltpu.CompilerParams(vmem_limit_bytes=16 << 20),
     )(pay)
 
 
 def shards(stacked, row_owner, dest_local):
     gram = local_gram(stacked)
     piece = lax.optimization_barrier(lax.psum_scatter(gram, "leaf", scatter_dimension=0, tiled=True))
-    half = SHARD // 2
-    g1 = lax.all_gather(piece[:half], "leaf", axis=0, tiled=True)
-    g2 = lax.all_gather(piece[half:SHARD], "leaf", axis=0, tiled=True)
+    groups = [list(range(first, NLEAF, 2)) for first in range(2)]
+    own = lax.all_gather(piece[:SHARD], "leaf", axis=0, tiled=True, axis_index_groups=groups)
+    half = NLEAF // 4 * SHARD
+    low = lax.ppermute(own[:half], "leaf", [(z, (z + 1) % NLEAF) for z in range(NLEAF)])
+    high = lax.ppermute(own[half:], "leaf", [(z, (z - 1) % NLEAF) for z in range(NLEAF)])
     owner = row_owner[0]
     dest = dest_local.reshape(CB_DEV, 1)
     leaf = lax.axis_index("leaf").astype(jnp.int32).reshape(1)
-    piv, pay = factor(g1, g2, owner.reshape(1, CB_DEV), owner, dest, leaf)
+    piv, pay = factor(own, low, high, owner.reshape(1, CB_DEV), owner, dest, leaf)
     got = lax.all_to_all(pay, "front", 0, 0, tiled=True)
     return piv, assemble(got)
 

time: 193 us -> 161 us (0.83)
  blocking collectives: 136 us -> 99.9 us
  Pallas kernels: 49.6 us -> 41.1 us
  starting transfers between devices: 2.98 us -> 9.47 us
  waiting for transfers between devices: 0.01 us -> 6.44 us
    all_gather x2 -> x1, blocking collectives: 58.4 us -> 29 us  [shards(): lax.all_gather(piece[:SHARD], 'leaf', axis=0, tiled=True, axis_index_grou...]
    pallas_call x1, Pallas kernels: 39.9 us -> 32.4 us  [factor(): pl.pallas_call(factor_kernel, out_shape=(jax.ShapeDtypeStruct((1, PIV //...]
    ppermute x0 -> x2, starting transfers between devices: none -> 6.49 us  [the longest x1 4.43 us: shards(): lax.ppermute(own[half:], 'leaf', [(z, (z - 1) % NLEAF) for z in range(NLE...]
    ppermute x0 -> x2, waiting for transfers between devices: none -> 6.43 us  [the longest x1 6.09 us: shards(): lax.ppermute(own[:half], 'leaf', [(z, (z + 1) % NLEAF) for z in range(NLE...]
    all_to_all x1, blocking collectives: 35.7 us -> 29.5 us  [shards(): got = lax.all_to_all(pay, 'front', 0, 0, tiled=True)]
  transfers between devices with their start and end apart: 1 -> 3, of which waited for: 0 -> 2; matrix products, arithmetic and copies ran while one was open for 1% -> 1% of each run, Pallas kernels for 0% -> 0%
where the time goes in v2:
time: 161 us; the launch traced here: 160 us
  blocking collectives  99.9 us (62%)
  Pallas kernels  41.1 us (26%)
  starting transfers between devices  9.47 us (6%)
  waiting for transfers between devices  6.44 us (4%)
  local copies, waits for them, and re-layouts  1.96 us (1%)
    unnamed x1, blocking collectives  41.4 us
    pallas_call x1, Pallas kernels, factor(): pl.pallas_call(factor_kernel, out_shape=(jax.ShapeDtypeStruct((1, PIV //...  32.4 us
    all_to_all x1, blocking collectives, shards(): got = lax.all_to_all(pay, 'front', 0, 0, tiled=True)  29.5 us
    all_gather x1, blocking collectives, shards(): lax.all_gather(piece[:SHARD], 'leaf', axis=0, tiled=True, axis_index_grou...  29 us
    pallas_call x1, Pallas kernels, local_gram(): pl.pallas_call(gram_kernel, out_shape=jax.ShapeDtypeStruct((NLEAF * PAD_S...  7.44 us
    ppermute x1, waiting for transfers between devices, shards(): lax.ppermute(own[:half], 'leaf', [(z, (z + 1) % NLEAF) for z in range(NLE...  6.09 us
    ppermute x1, starting transfers between devices, shards(): lax.ppermute(own[half:], 'leaf', [(z, (z - 1) % NLEAF) for z in range(NLE...  4.43 us
  transfers between devices with their start and end apart: 3, of which 2 were waited for; matrix products, arithmetic and copies ran while one was open for 1% of the time, Pallas kernels for 0%

profile of v2, /device:TPU:1, one launch (start us, length us, event | category | flops | bytes accessed | tf_op | source)
XLA Modules:
  0.0 160.3 jit_solution(647553366142012873)
XLA Ops:
  0.6 7.4 %local_gram.1 = f32[3600,128]{1,0:T(8,128)} custom-call(f32[1,1024,896]{2,1,0:T(8,128)} %x_ref.1), custom_call_target="tpu_custom_call" | custom-call | tf_op jit(solution)/shard_map/local_gram/pallas_call | solution.py:79
  8.1 41.4 %fusion = f32[240,128]{1,0:T(8,128)S(1)} fusion(f32[3600,128]{1,0:T(8,128)} %local_gram.1), kind=kCustom, calls=%all-reduce-scatter | all-reduce-scatter fusion | flops 491521 | bytes 1968128
  49.5 0.0 copy-start
  49.5 0.0 copy-start.1
  49.5 3.0 %collective-permute-start.2 = (f32[225,128]{1,0:T(8,128)S(1)}, f32[225,128]{1,0:T(8,128)S(1)}, u32[]{:S(2)}, u32[]{:S(2)}) collective-permute-start(f32[225,128]{1,0:T(8,128)S(1)} %slice.15), channel_id=1, source_target_pairs={{0,32},{32,64},{64,96},{96,128},{128,160},{160,192},{192,224},{224... | collective-permute-start | bytes 345608
  52.5 1.3 dynamic-slice.4
  54.4 0.0 collective-permute-done.2
  54.4 0.4 concatenate
  54.9 29.0 %all_gather.3.g_ref = f32[1792,128]{1,0:T(8,128)S(1)} all-gather(f32[224,128]{1,0:T(8,128)S(1)} %slice.12), channel_id=1, replica_groups={{0,64,128,192,256,320,384,448},{32,96,160,224,288,352,416,480},{1,65,12..., dimensions={0}, use_global_device_ids=true | all-gather | bytes 1032192 | tf_op jit(solution)/shard_map/all_gather | solution.py:259
  83.8 0.1 fusion.1
  83.9 2.1 %collective-permute-start = (f32[896,128]{1,0:T(8,128)S(1)}, f32[896,128]{1,0:T(8,128)S(1)}, u32[]{:S(2)}, u32[]{:S(2)}) collective-permute-start(f32[896,128]{1,0:T(8,128)S(1)} %get-tuple-element.7), channel_id=1, source_target_pairs={{0,32},{32,64},{64,96},{96,128},{128,160},{160,192},{192,224},{224... | collective-permute-start | bytes 1376264 | tf_op jit(solution)/shard_map/ppermute | solution.py:261
  86.0 4.4 %collective-permute-start.1 = (f32[896,128]{1,0:T(8,128)S(1)}, f32[896,128]{1,0:T(8,128)S(1)}, u32[]{:S(2)}, u32[]{:S(2)}) collective-permute-start(f32[896,128]{1,0:T(8,128)S(1)} %get-tuple-element.6), channel_id=1, source_target_pairs={{0,480},{32,0},{64,32},{96,64},{128,96},{160,128},{192,160},{224,1... | collective-permute-start | bytes 1376264 | tf_op jit(solution)/shard_map/ppermute | solution.py:262
  90.4 0.0 copy-done
  90.4 0.1 copy.7.owner_ref
  90.5 0.0 copy-done.1
  90.5 0.1 copy.8.dest_ref
  90.6 6.1 %collective-permute-done.low_ref = f32[896,128]{1,0:T(8,128)S(1)} collective-permute-done((f32[896,128]{1,0:T(8,128)S(1)}, f32[896,128]{1,0:T(8,128)S(1)}, u32[]{:S(2)}, u32[]{:S(2)}) %collective-permute-start) | collective-permute-done | bytes 458784 | tf_op jit(solution)/shard_map/ppermute | solution.py:261
  96.7 0.3 collective-permute-done.1.high_ref
  97.0 32.4 %factor.1 = (f32[1,16,896]{2,1,0:T(8,128)}, f32[512,128]{1,0:T(8,128)S(1)}) custom-call(f32[1792,128]{1,0:T(8,128)S(1)} %all_gather.3.g_ref, f32[896,128]{1,0:T(8,128)S(1)} %collective-permute-done.low_ref, f32[896,128]{1,0:T(8,128)S(1)} %collective-permute-done.1.high_ref, s32[1,40]{1,0:T(1,128)S(1)} %bitcast.12, s32[40,1]{1,0:T(8,128)S(1)} %copy.7.owner_ref, ...), custom_call_target="tpu_custom_call" | custom-call | tf_op jit(solution)/shard_map/factor/pallas_call | solution.py:214
  129.4 29.5 %all_to_all.11 = f32[32,16,128]{2,1,0:T(8,128)S(1)} all-to-all(f32[32,16,128]{2,1,0:T(8,128)S(1)} %bitcast.10), channel_id=1, replica_groups=mesh['leaf'=16,'front'=32] {'front'}, dimensions={0} | all-to-all | bytes 524288 | tf_op jit(solution)/shard_map/all_to_all | solution.py:267
  158.9 1.3 assemble.1
  (3 shorter events, 0.0 us)
Async XLA Ops:
  49.5 40.9 %copy-start = (s32[1,40,1]{1,2,0:T(1,128)S(1)}, s32[1,40,1]{1,2,0:T(1,128)}, u32[]{:S(2)}) copy-start(s32[1,40,1]{1,2,0:T(1,128)} %param.4) | copy-start | bytes 484
  49.5 41.0 %copy-start.1 = (s32[1,40]{1,0:T(1,128)S(1)}, s32[1,40]{1,0:T(1,128)}, u32[]{:S(2)}) copy-start(s32[1,40]{1,0:T(1,128)} %param.5) | copy-start | bytes 484
  49.5 4.9 %collective-permute-start.2 = (f32[225,128]{1,0:T(8,128)S(1)}, f32[225,128]{1,0:T(8,128)S(1)}, u32[]{:S(2)}, u32[]{:S(2)}) collective-permute-start(f32[225,128]{1,0:T(8,128)S(1)} %slice.15), channel_id=1, source_target_pairs={{0,32},{32,64},{64,96},{96,128},{128,160},{160,192},{192,224},{224... | collective-permute-start | bytes 345608
  83.9 12.8 %collective-permute-start = (f32[896,128]{1,0:T(8,128)S(1)}, f32[896,128]{1,0:T(8,128)S(1)}, u32[]{:S(2)}, u32[]{:S(2)}) collective-permute-start(f32[896,128]{1,0:T(8,128)S(1)} %get-tuple-element.7), channel_id=1, source_target_pairs={{0,32},{32,64},{64,96},{96,128},{128,160},{160,192},{192,224},{224... | collective-permute-start | bytes 1376264 | tf_op jit(solution)/shard_map/ppermute | solution.py:261
  86.0 11.1 %collective-permute-start.1 = (f32[896,128]{1,0:T(8,128)S(1)}, f32[896,128]{1,0:T(8,128)S(1)}, u32[]{:S(2)}, u32[]{:S(2)}) collective-permute-start(f32[896,128]{1,0:T(8,128)S(1)} %get-tuple-element.6), channel_id=1, source_target_pairs={{0,480},{32,0},{64,32},{96,64},{128,96},{160,128},{192,160},{224,1... | collective-permute-start | bytes 1376264 | tf_op jit(solution)/shard_map/ppermute | solution.py:262

commit v3 on v2

--- a/solution.py
+++ b/solution.py
@@ -17,10 +17,12 @@
 SUB = 8
 NLEAF = 16
 NFRONT = 32
-PACKED = NT * (NT + 1) // 2 * T
-SHARD = PACKED // NLEAF
-PAD_SHARD = SHARD + 1
-UNIT = 16
+PAIRS = ((0, 1), (2, 3), (4, 5))
+LONE = NT - 1
+TILES = NT * (NT + 1) // 2
+FULL = (TILES - len(PAIRS)) * T
+SHARD = 201
+HALF = NLEAF // 4
 F32 = jnp.float32
 BF16 = jnp.bfloat16
 HIGHEST = lax.Precision.HIGHEST
@@ -28,6 +30,23 @@
 
 def tile_index(i, j):
     return i * NT - i * (i - 1) // 2 + (j - i)
+
+
+def packed_tiles():
+    order = [(i, j) for i in range(NT) for j in range(i + 1, NT)]
+    return order + [(LONE, LONE)] + [(p, p) for p, _ in PAIRS]
+
+
+def pieces(start, stop):
+    while start < stop:
+        chunk, rest = divmod(start, SHARD)
+        size = min(stop - start, SHARD - rest)
+        yield start, chunk, rest, size
+        start += size
+
+
+def square_iota(axis):
+    return lax.broadcasted_iota(jnp.int32, (T, T), axis)
 
 
 def halves(x):
@@ -68,21 +87,35 @@
 
     @pl.when(step == pl.num_programs(0) - 1)
     def _():
-        for z in range(NLEAF):
-            out_ref[z * PAD_SHARD : z * PAD_SHARD + SHARD, :] = acc_ref[z * SHARD : (z + 1) * SHARD, :]
-            out_ref[z * PAD_SHARD + SHARD : (z + 1) * PAD_SHARD, :] = jnp.zeros((PAD_SHARD - SHARD, T), F32)
+        def tile(i, j):
+            row = tile_index(i, j) * T
+            return acc_ref[row : row + T, :]
+
+        row, col = square_iota(0), square_iota(1)
+        partner = dict(PAIRS)
+        for n, (i, j) in enumerate(packed_tiles()):
+            value = tile(i, j)
+            if i == j and i in partner:
+                q = partner[i]
+                other = tile(q, q)
+                value = jnp.where(row <= col, value, other)
+                at = FULL + PAIRS.index((i, q))
+                out_ref[at : at + 1, :] = jnp.sum(jnp.where(row == col, other, 0.0), axis=0, keepdims=True)
+            out_ref[n * T : (n + 1) * T, :] = value
+        spare = FULL + len(PAIRS)
+        out_ref[spare : NLEAF * SHARD, :] = jnp.zeros((NLEAF * SHARD - spare, T), F32)
 
 
 def local_gram(stacked):
     rows = stacked.shape[1]
-    chunk = 256
+    chunk = 512
     return pl.pallas_call(
         gram_kernel,
-        out_shape=jax.ShapeDtypeStruct((NLEAF * PAD_SHARD, T), F32),
+        out_shape=jax.ShapeDtypeStruct((NLEAF * SHARD, T), F32),
         grid=(rows // chunk,),
         in_specs=[pl.BlockSpec((1, chunk, COLS), lambda k: (0, k, 0))],
-        out_specs=pl.BlockSpec((NLEAF * PAD_SHARD, T), lambda k: (0, 0)),
-        scratch_shapes=[pltpu.VMEM((PACKED, T), F32)],
+        out_specs=pl.BlockSpec((NLEAF * SHARD, T), lambda k: (0, 0)),
+        scratch_shapes=[pltpu.VMEM((TILES * T, T), F32)],
         name="local_gram",
         compiler_params=pltpu.CompilerParams(vmem_limit_bytes=61 << 20),
     )(stacked)
@@ -108,10 +141,13 @@
         col = [lanes_of(rows[b], c0 + k) for k in range(SUB)]
         work = jnp.where(inside, (lane == sub + c0).astype(F32), rows[b])
         done = jnp.zeros((SUB, T), F32)
+        pivot = row_of(col[0], 0)
         for k in range(SUB):
-            root = lax.rsqrt(row_of(col[k], k))
+            root = lax.rsqrt(pivot)
             inverse = root * root
             ahead = [row_of(col[j], k) if j > k else None for j in range(SUB)]
+            if k + 1 < SUB:
+                pivot = row_of(col[k + 1], k + 1) - (ahead[k + 1] * ahead[k + 1]) * inverse
             for j in range(k + 1, SUB):
                 prod = col[k] * ahead[j]
                 col[j] = jnp.where(is_row[k], ahead[j] * inverse, col[j] - prod * inverse)
@@ -150,23 +186,34 @@
             d_ref[...] = block[:, :T]
 
 
-def unpack(mine, parity, g_ref, low_ref, high_ref, s_ref):
-    per = SHARD // UNIT
-    for i in range(NT):
-        for j in range(i, NT):
-            for u in range(T // UNIT):
-                z, rest = divmod(tile_index(i, j) * (T // UNIT) + u, per)
-                if (z % 2 == parity) != mine:
-                    continue
-                row = (z // 2 * per + rest) * UNIT
-                src = g_ref
-                if not mine:
-                    half = NLEAF // 4 * SHARD
-                    src, row = (low_ref, row) if row < half else (high_ref, row - half)
-                s_ref[i * T + u * UNIT : i * T + (u + 1) * UNIT, j * T : (j + 1) * T] = src[row : row + UNIT, :]
-
-
-def factor_kernel(g_ref, low_ref, high_ref, owner_row_ref, owner_ref, dest_ref, leaf_ref, piv_ref, pay_ref, s_ref, d_ref, inv_ref):
+def unpack(parity, g_ref, low_ref, high_ref, s_ref, diag_ref):
+    def move(dst, row, col, start, stop):
+        for first, chunk, rest, size in pieces(start, stop):
+            member = chunk // 2
+            src = g_ref
+            if chunk % 2 != parity:
+                src, member = (low_ref, member) if member < HALF else (high_ref, member - HALF)
+            to = row + first - start
+            dst[to : to + size, col : col + T] = src[member, rest : rest + size, :]
+
+    for n, (i, j) in enumerate(packed_tiles()):
+        move(s_ref, i * T, j * T, n * T, (n + 1) * T)
+    move(diag_ref, 0, 0, FULL, FULL + len(PAIRS))
+
+
+def split_pairs(s_ref, diag_ref):
+    row, col = square_iota(0), square_iota(1)
+    for n, (p, q) in enumerate(PAIRS):
+        both = s_ref[p * T : (p + 1) * T, p * T : (p + 1) * T]
+        turned = jnp.transpose(both)
+        s_ref[p * T : (p + 1) * T, p * T : (p + 1) * T] = jnp.where(row <= col, both, turned)
+        other = jnp.where(row > col, both, turned)
+        s_ref[q * T : (q + 1) * T, q * T : (q + 1) * T] = jnp.where(
+            row == col, jnp.broadcast_to(diag_ref[n : n + 1, :], (T, T)), other
+        )
+
+
+def factor_kernel(g_ref, low_ref, high_ref, owner_row_ref, owner_ref, dest_ref, leaf_ref, piv_ref, pay_ref, s_ref, d_ref, inv_ref, diag_ref):
     for i in range(NT):
         for j in range(i):
             s_ref[i * T : (i + 1) * T, j * T : (j + 1) * T] = jnp.zeros((T, T), F32)
@@ -175,9 +222,9 @@
 
         @pl.when(lax.rem(leaf, 2) == parity)
         def _():
-            for mine in (True, False):
-                unpack(mine, parity, g_ref, low_ref, high_ref, s_ref)
-
+            unpack(parity, g_ref, low_ref, high_ref, s_ref, diag_ref)
+
+    split_pairs(s_ref, diag_ref)
     d_ref[...] = s_ref[:T, :T]
 
     def panel_step(p, _):
@@ -219,7 +266,7 @@
         ),
         in_specs=[vmem] * 6 + [pl.BlockSpec(memory_space=pltpu.SMEM)],
         out_specs=(vmem, vmem),
-        scratch_shapes=[pltpu.VMEM((COLS, COLS), F32), pltpu.VMEM((T, T), F32), pltpu.VMEM((T, T), F32)],
+        scratch_shapes=[pltpu.VMEM((COLS, COLS), F32), pltpu.VMEM((T, T), F32), pltpu.VMEM((T, T), F32), pltpu.VMEM((8, T), F32)],
         name="factor",
         compiler_params=pltpu.CompilerParams(vmem_limit_bytes=24 << 20),
     )(g, low, high, owner_row, owner, dest, leaf)
@@ -256,10 +303,9 @@
     gram = local_gram(stacked)
     piece = lax.optimization_barrier(lax.psum_scatter(gram, "leaf", scatter_dimension=0, tiled=True))
     groups = [list(range(first, NLEAF, 2)) for first in range(2)]
-    own = lax.all_gather(piece[:SHARD], "leaf", axis=0, tiled=True, axis_index_groups=groups)
-    half = NLEAF // 4 * SHARD
-    low = lax.ppermute(own[:half], "leaf", [(z, (z + 1) % NLEAF) for z in range(NLEAF)])
-    high = lax.ppermute(own[half:], "leaf", [(z, (z - 1) % NLEAF) for z in range(NLEAF)])
+    own = lax.all_gather(piece, "leaf", axis=0, axis_index_groups=groups)
+    low = lax.ppermute(own[:HALF], "leaf", [(z, (z + 1) % NLEAF) for z in range(NLEAF)])
+    high = lax.ppermute(own[HALF:], "leaf", [(z, (z - 1) % NLEAF) for z in range(NLEAF)])
     owner = row_owner[0]
     dest = dest_local.reshape(CB_DEV, 1)
     leaf = lax.axis_index("leaf").astype(jnp.int32).reshape(1)

time: 161 us -> 153 us (0.950)
  Pallas kernels: 41.1 us -> 36.8 us
  blocking collectives: 99.9 us -> 98.2 us
    pallas_call x1, Pallas kernels: 32.4 us -> 28.2 us  [factor(): pl.pallas_call(factor_kernel, out_shape=(jax.ShapeDtypeStruct((1, PIV //...]
where the time goes in v3:
time: 153 us
  blocking collectives  98.2 us (64%)
  Pallas kernels  36.8 us (24%)
  starting transfers between devices  8.79 us (6%)
  waiting for transfers between devices  6 us (4%)
  local copies, waits for them, and re-layouts  1.92 us (1%)
    unnamed x1, blocking collectives  39.8 us
    all_gather x1, blocking collectives, shards(): own = lax.all_gather(piece, 'leaf', axis=0, axis_index_groups=groups)  29.6 us
    all_to_all x1, blocking collectives, shards(): got = lax.all_to_all(pay, 'front', 0, 0, tiled=True)  28.8 us
    pallas_call x1, Pallas kernels, factor(): pl.pallas_call(factor_kernel, out_shape=(jax.ShapeDtypeStruct((1, PIV //...  28.2 us
    pallas_call x1, Pallas kernels, local_gram(): pl.pallas_call(gram_kernel, out_shape=jax.ShapeDtypeStruct((NLEAF * SHARD...  7.23 us
    ppermute x1, waiting for transfers between devices, shards(): lax.ppermute(own[:HALF], 'leaf', [(z, (z + 1) % NLEAF) for z in range(NLE...  5.65 us
    ppermute x1, starting transfers between devices, shards(): lax.ppermute(own[HALF:], 'leaf', [(z, (z - 1) % NLEAF) for z in range(NLE...  4.57 us
  transfers between devices with their start and end apart: 3, of which 2 were waited for; matrix products, arithmetic and copies ran while one was open for 1% of the time, Pallas kernels for 0%

profile of v3, /device:TPU:1, one launch (start us, length us, event | category | flops | bytes accessed | tf_op | source)
XLA Modules:
  0.0 153.1 jit_solution(9901902831167443773)
XLA Ops:
  0.6 7.2 %local_gram.1 = f32[3216,128]{1,0:T(8,128)} custom-call(f32[1,1024,896]{2,1,0:T(8,128)} %x_ref.1), custom_call_target="tpu_custom_call" | custom-call | tf_op jit(solution)/shard_map/local_gram/pallas_call | solution.py:112
  7.9 39.8 %fusion = f32[208,128]{1,0:T(8,128)S(1)} fusion(f32[3216,128]{1,0:T(8,128)} %local_gram.1), kind=kCustom, calls=%all-reduce-scatter | all-reduce-scatter fusion | flops 425985 | bytes 1755136
  47.6 0.0 copy-start
  47.7 0.0 copy-start.1
  47.7 2.3 %collective-permute-start.2 = (f32[105,128]{1,0:T(8,128)S(1)}, f32[105,128]{1,0:T(8,128)S(1)}, u32[]{:S(2)}, u32[]{:S(2)}) collective-permute-start(f32[105,128]{1,0:T(8,128)S(1)} %slice.14), channel_id=1, source_target_pairs={{0,32},{32,64},{64,96},{96,128},{128,160},{160,192},{192,224},{224... | collective-permute-start | bytes 161288
  50.0 1.3 dynamic-slice.4
  51.9 0.0 collective-permute-done.2
  51.9 0.4 concatenate
  52.3 29.6 %all-gather.1.g_ref = f32[8,201,128]{2,1,0:T(8,128)S(1)} all-gather(f32[1,201,128]{2,1,0:T(8,128)S(1)} %bitcast.14), channel_id=2, replica_groups={{0,64,128,192,256,320,384,448},{32,96,160,224,288,352,416,480},{1,65,12..., dimensions={0}, use_global_device_ids=true | all-gather | bytes 926208 | tf_op jit(solution)/shard_map/all_gather | solution.py:306
  81.9 0.1 fusion.1
  82.0 1.9 %collective-permute-start = (f32[4,201,128]{2,1,0:T(8,128)S(1)}, f32[4,201,128]{2,1,0:T(8,128)S(1)}, u32[]{:S(2)}, u32[]{:S(2)}) collective-permute-start(f32[4,201,128]{2,1,0:T(8,128)S(1)} %get-tuple-element.7), channel_id=1, source_target_pairs={{0,32},{32,64},{64,96},{96,128},{128,160},{160,192},{192,224},{224... | collective-permute-start | bytes 1234952 | tf_op jit(solution)/shard_map/ppermute | solution.py:307
  83.9 4.6 %collective-permute-start.1 = (f32[4,201,128]{2,1,0:T(8,128)S(1)}, f32[4,201,128]{2,1,0:T(8,128)S(1)}, u32[]{:S(2)}, u32[]{:S(2)}) collective-permute-start(f32[4,201,128]{2,1,0:T(8,128)S(1)} %get-tuple-element.6), channel_id=1, source_target_pairs={{0,480},{32,0},{64,32},{96,64},{128,96},{160,128},{192,160},{224,1... | collective-permute-start | bytes 1234952 | tf_op jit(solution)/shard_map/ppermute | solution.py:308
  88.5 0.0 copy-done
  88.5 0.1 copy.7.owner_ref
  88.6 0.0 copy-done.1
  88.6 0.1 copy.8.dest_ref
  88.7 5.6 %collective-permute-done.low_ref = f32[4,201,128]{2,1,0:T(8,128)S(1)} collective-permute-done((f32[4,201,128]{2,1,0:T(8,128)S(1)}, f32[4,201,128]{2,1,0:T(8,128)S(1)}, u32[]{:S(2)}, u32[]{:S(2)}) %collective-permute-start) | collective-permute-done | bytes 411680 | tf_op jit(solution)/shard_map/ppermute | solution.py:307
  94.3 0.3 collective-permute-done.1.high_ref
  94.7 28.2 %factor.1 = (f32[1,16,896]{2,1,0:T(8,128)}, f32[512,128]{1,0:T(8,128)S(1)}) custom-call(f32[8,201,128]{2,1,0:T(8,128)S(1)} %all-gather.1.g_ref, f32[4,201,128]{2,1,0:T(8,128)S(1)} %collective-permute-done.low_ref, f32[4,201,128]{2,1,0:T(8,128)S(1)} %collective-permute-done.1.high_ref, s32[1,40]{1,0:T(1,128)S(1)} %bitcast.13, s32[40,1]{1,0:T(8,128)S(1)} %copy.7.owner_ref, ...), custom_call_target="tpu_custom_call" | custom-call | tf_op jit(solution)/shard_map/factor/pallas_call | solution.py:261
  122.9 28.8 %all_to_all.11 = f32[32,16,128]{2,1,0:T(8,128)S(1)} all-to-all(f32[32,16,128]{2,1,0:T(8,128)S(1)} %bitcast.11), channel_id=1, replica_groups=mesh['leaf'=16,'front'=32] {'front'}, dimensions={0} | all-to-all | bytes 524288 | tf_op jit(solution)/shard_map/all_to_all | solution.py:313
  151.7 1.3 assemble.1
  (2 shorter events, 0.0 us)
Async XLA Ops:
  47.6 40.8 %copy-start = (s32[1,40,1]{1,2,0:T(1,128)S(1)}, s32[1,40,1]{1,2,0:T(1,128)}, u32[]{:S(2)}) copy-start(s32[1,40,1]{1,2,0:T(1,128)} %param.4) | copy-start | bytes 484
  47.7 40.9 %copy-start.1 = (s32[1,40]{1,0:T(1,128)S(1)}, s32[1,40]{1,0:T(1,128)}, u32[]{:S(2)}) copy-start(s32[1,40]{1,0:T(1,128)} %param.5) | copy-start | bytes 484
  47.7 4.2 %collective-permute-start.2 = (f32[105,128]{1,0:T(8,128)S(1)}, f32[105,128]{1,0:T(8,128)S(1)}, u32[]{:S(2)}, u32[]{:S(2)}) collective-permute-start(f32[105,128]{1,0:T(8,128)S(1)} %slice.14), channel_id=1, source_target_pairs={{0,32},{32,64},{64,96},{96,128},{128,160},{160,192},{192,224},{224... | collective-permute-start | bytes 161288
  82.0 12.4 %collective-permute-start = (f32[4,201,128]{2,1,0:T(8,128)S(1)}, f32[4,201,128]{2,1,0:T(8,128)S(1)}, u32[]{:S(2)}, u32[]{:S(2)}) collective-permute-start(f32[4,201,128]{2,1,0:T(8,128)S(1)} %get-tuple-element.7), channel_id=1, source_target_pairs={{0,32},{32,64},{64,96},{96,128},{128,160},{160,192},{192,224},{224... | collective-permute-start | bytes 1234952 | tf_op jit(solution)/shard_map/ppermute | solution.py:307
  83.9 10.8 %collective-permute-start.1 = (f32[4,201,128]{2,1,0:T(8,128)S(1)}, f32[4,201,128]{2,1,0:T(8,128)S(1)}, u32[]{:S(2)}, u32[]{:S(2)}) collective-permute-start(f32[4,201,128]{2,1,0:T(8,128)S(1)} %get-tuple-element.6), channel_id=1, source_target_pairs={{0,480},{32,0},{64,32},{96,64},{128,96},{160,128},{192,160},{224,1... | collective-permute-start | bytes 1234952 | tf_op jit(solution)/shard_map/ppermute | solution.py:308

commit v4 on v3

--- a/solution.py
+++ b/solution.py
@@ -135,26 +135,39 @@
     is_row = [sub == k for k in range(SUB)]
     nb = T // SUB
     rows = [d_ref[SUB * i : SUB * (i + 1), :] for i in range(nb)]
+    start = list(rows)
     for b in range(nb):
         c0 = SUB * b
         inside = (lane >= c0) & (lane < c0 + SUB)
         col = [lanes_of(rows[b], c0 + k) for k in range(SUB)]
         work = jnp.where(inside, (lane == sub + c0).astype(F32), rows[b])
         done = jnp.zeros((SUB, T), F32)
-        pivot = row_of(col[0], 0)
-        for k in range(SUB):
+        first = [row_of(lanes_of(start[b], c0 + k), k) for k in range(0, SUB, 2)]
+        scale = [lax.rsqrt(v) for v in first]
+        scale = [v * v for v in scale]
+        pivot, cross, partner = row_of(col[0], 0), row_of(col[1], 0), row_of(col[1], 1)
+        for k in range(0, SUB, 2):
+            share = pivot * scale[k // 2]
+            det = partner * share - cross * (cross * scale[k // 2])
+            root_det = lax.rsqrt(det)
             root = lax.rsqrt(pivot)
             inverse = root * root
-            ahead = [row_of(col[j], k) if j > k else None for j in range(SUB)]
-            if k + 1 < SUB:
-                pivot = row_of(col[k + 1], k + 1) - (ahead[k + 1] * ahead[k + 1]) * inverse
-            for j in range(k + 1, SUB):
-                prod = col[k] * ahead[j]
-                col[j] = jnp.where(is_row[k], ahead[j] * inverse, col[j] - prod * inverse)
-            rk = row_of(work, k)
-            done = jnp.where(is_row[k], rk * root, done)
-            pk = rk * inverse
-            work = jnp.where(is_row[k], pk, work - col[k] * pk)
+            second = root_det * root_det * share
+            second_root = root_det * (share * lax.rsqrt(share))
+            for q, (one, two) in ((k, (root, inverse)), (k + 1, (second_root, second))):
+                ahead = [row_of(col[j], q) if j > q else None for j in range(SUB)]
+                if q > k and q + 1 < SUB:
+                    near, far = ahead[q + 1], ahead[q + 2]
+                    pivot = row_of(col[q + 1], q + 1) - (near * near) * two
+                    cross = row_of(col[q + 2], q + 1) - (near * far) * two
+                    partner = row_of(col[q + 2], q + 2) - (far * far) * two
+                for j in range(q + 1, SUB):
+                    prod = col[q] * ahead[j]
+                    col[j] = jnp.where(is_row[q], ahead[j] * two, col[j] - prod * two)
+                rk = row_of(work, q)
+                done = jnp.where(is_row[q], rk * one, done)
+                pk = rk * two
+                work = jnp.where(is_row[q], pk, work - col[q] * pk)
         inv_ref[c0 : c0 + SUB, :] = jnp.where(lane < c0 + SUB, done, 0.0)
         if b + 1 < nb:
             solved = [row_of(work, k) for k in range(SUB)]

time: 153 us -> 152 us (level)
  Pallas kernels: 36.8 us -> 35.2 us
    pallas_call x1, Pallas kernels: 28.2 us -> 26.6 us  [factor(): pl.pallas_call(factor_kernel, out_shape=(jax.ShapeDtypeStruct((1, PIV //...]
where the time goes in v4:
time: 152 us; the launch traced here: 151 us
  blocking collectives  98.2 us (65%)
  Pallas kernels  35.2 us (23%)
  starting transfers between devices  8.79 us (6%)
  waiting for transfers between devices  6 us (4%)
  local copies, waits for them, and re-layouts  1.92 us (1%)
    unnamed x1, blocking collectives  39.8 us
    all_gather x1, blocking collectives, shards(): own = lax.all_gather(piece, 'leaf', axis=0, axis_index_groups=groups)  29.6 us
    all_to_all x1, blocking collectives, shards(): got = lax.all_to_all(pay, 'front', 0, 0, tiled=True)  28.8 us
    pallas_call x1, Pallas kernels, factor(): pl.pallas_call(factor_kernel, out_shape=(jax.ShapeDtypeStruct((1, PIV //...  26.6 us
    pallas_call x1, Pallas kernels, local_gram(): pl.pallas_call(gram_kernel, out_shape=jax.ShapeDtypeStruct((NLEAF * SHARD...  7.23 us
    ppermute x1, waiting for transfers between devices, shards(): lax.ppermute(own[:HALF], 'leaf', [(z, (z + 1) % NLEAF) for z in range(NLE...  5.65 us
    ppermute x1, starting transfers between devices, shards(): lax.ppermute(own[HALF:], 'leaf', [(z, (z - 1) % NLEAF) for z in range(NLE...  4.57 us
  transfers between devices with their start and end apart: 3, of which 2 were waited for; matrix products, arithmetic and copies ran while one was open for 1% of the time, Pallas kernels for 0%

profile of v4, /device:TPU:1, one launch (start us, length us, event | category | flops | bytes accessed | tf_op | source)
XLA Modules:
  0.0 151.4 jit_solution(11934730427188474853)
XLA Ops:
  0.6 7.2 %local_gram.1 = f32[3216,128]{1,0:T(8,128)} custom-call(f32[1,1024,896]{2,1,0:T(8,128)} %x_ref.1), custom_call_target="tpu_custom_call" | custom-call | tf_op jit(solution)/shard_map/local_gram/pallas_call | solution.py:112
  7.9 39.8 %fusion = f32[208,128]{1,0:T(8,128)S(1)} fusion(f32[3216,128]{1,0:T(8,128)} %local_gram.1), kind=kCustom, calls=%all-reduce-scatter | all-reduce-scatter fusion | flops 425985 | bytes 1755136
  47.6 0.0 copy-start
  47.7 0.0 copy-start.1
  47.7 2.3 %collective-permute-start.2 = (f32[105,128]{1,0:T(8,128)S(1)}, f32[105,128]{1,0:T(8,128)S(1)}, u32[]{:S(2)}, u32[]{:S(2)}) collective-permute-start(f32[105,128]{1,0:T(8,128)S(1)} %slice.14), channel_id=1, source_target_pairs={{0,32},{32,64},{64,96},{96,128},{128,160},{160,192},{192,224},{224... | collective-permute-start | bytes 161288
  50.0 1.3 dynamic-slice.4
  51.9 0.0 collective-permute-done.2
  51.9 0.4 concatenate
  52.3 29.6 %all-gather.1.g_ref = f32[8,201,128]{2,1,0:T(8,128)S(1)} all-gather(f32[1,201,128]{2,1,0:T(8,128)S(1)} %bitcast.14), channel_id=2, replica_groups={{0,64,128,192,256,320,384,448},{32,96,160,224,288,352,416,480},{1,65,12..., dimensions={0}, use_global_device_ids=true | all-gather | bytes 926208 | tf_op jit(solution)/shard_map/all_gather | solution.py:319
  81.9 0.1 fusion.1
  82.0 1.9 %collective-permute-start = (f32[4,201,128]{2,1,0:T(8,128)S(1)}, f32[4,201,128]{2,1,0:T(8,128)S(1)}, u32[]{:S(2)}, u32[]{:S(2)}) collective-permute-start(f32[4,201,128]{2,1,0:T(8,128)S(1)} %get-tuple-element.7), channel_id=1, source_target_pairs={{0,32},{32,64},{64,96},{96,128},{128,160},{160,192},{192,224},{224... | collective-permute-start | bytes 1234952 | tf_op jit(solution)/shard_map/ppermute | solution.py:320
  83.9 4.6 %collective-permute-start.1 = (f32[4,201,128]{2,1,0:T(8,128)S(1)}, f32[4,201,128]{2,1,0:T(8,128)S(1)}, u32[]{:S(2)}, u32[]{:S(2)}) collective-permute-start(f32[4,201,128]{2,1,0:T(8,128)S(1)} %get-tuple-element.6), channel_id=1, source_target_pairs={{0,480},{32,0},{64,32},{96,64},{128,96},{160,128},{192,160},{224,1... | collective-permute-start | bytes 1234952 | tf_op jit(solution)/shard_map/ppermute | solution.py:321
  88.5 0.0 copy-done
  88.5 0.1 copy.7.owner_ref
  88.6 0.0 copy-done.1
  88.6 0.1 copy.8.dest_ref
  88.7 5.6 %collective-permute-done.low_ref = f32[4,201,128]{2,1,0:T(8,128)S(1)} collective-permute-done((f32[4,201,128]{2,1,0:T(8,128)S(1)}, f32[4,201,128]{2,1,0:T(8,128)S(1)}, u32[]{:S(2)}, u32[]{:S(2)}) %collective-permute-start) | collective-permute-done | bytes 411680 | tf_op jit(solution)/shard_map/ppermute | solution.py:320
  94.3 0.3 collective-permute-done.1.high_ref
  94.7 26.6 %factor.1 = (f32[1,16,896]{2,1,0:T(8,128)}, f32[512,128]{1,0:T(8,128)S(1)}) custom-call(f32[8,201,128]{2,1,0:T(8,128)S(1)} %all-gather.1.g_ref, f32[4,201,128]{2,1,0:T(8,128)S(1)} %collective-permute-done.low_ref, f32[4,201,128]{2,1,0:T(8,128)S(1)} %collective-permute-done.1.high_ref, s32[1,40]{1,0:T(1,128)S(1)} %bitcast.13, s32[40,1]{1,0:T(8,128)S(1)} %copy.7.owner_ref, ...), custom_call_target="tpu_custom_call" | custom-call | tf_op jit(solution)/shard_map/factor/pallas_call | solution.py:274
  121.3 28.8 %all_to_all.11 = f32[32,16,128]{2,1,0:T(8,128)S(1)} all-to-all(f32[32,16,128]{2,1,0:T(8,128)S(1)} %bitcast.11), channel_id=1, replica_groups=mesh['leaf'=16,'front'=32] {'front'}, dimensions={0} | all-to-all | bytes 524288 | tf_op jit(solution)/shard_map/all_to_all | solution.py:326
  150.1 1.3 assemble.1
  (2 shorter events, 0.0 us)
Async XLA Ops:
  47.6 40.8 %copy-start = (s32[1,40,1]{1,2,0:T(1,128)S(1)}, s32[1,40,1]{1,2,0:T(1,128)}, u32[]{:S(2)}) copy-start(s32[1,40,1]{1,2,0:T(1,128)} %param.4) | copy-start | bytes 484
  47.7 40.9 %copy-start.1 = (s32[1,40]{1,0:T(1,128)S(1)}, s32[1,40]{1,0:T(1,128)}, u32[]{:S(2)}) copy-start(s32[1,40]{1,0:T(1,128)} %param.5) | copy-start | bytes 484
  47.7 4.2 %collective-permute-start.2 = (f32[105,128]{1,0:T(8,128)S(1)}, f32[105,128]{1,0:T(8,128)S(1)}, u32[]{:S(2)}, u32[]{:S(2)}) collective-permute-start(f32[105,128]{1,0:T(8,128)S(1)} %slice.14), channel_id=1, source_target_pairs={{0,32},{32,64},{64,96},{96,128},{128,160},{160,192},{192,224},{224... | collective-permute-start | bytes 161288
  82.0 12.4 %collective-permute-start = (f32[4,201,128]{2,1,0:T(8,128)S(1)}, f32[4,201,128]{2,1,0:T(8,128)S(1)}, u32[]{:S(2)}, u32[]{:S(2)}) collective-permute-start(f32[4,201,128]{2,1,0:T(8,128)S(1)} %get-tuple-element.7), channel_id=1, source_target_pairs={{0,32},{32,64},{64,96},{96,128},{128,160},{160,192},{192,224},{224... | collective-permute-start | bytes 1234952 | tf_op jit(solution)/shard_map/ppermute | solution.py:320
  83.9 10.8 %collective-permute-start.1 = (f32[4,201,128]{2,1,0:T(8,128)S(1)}, f32[4,201,128]{2,1,0:T(8,128)S(1)}, u32[]{:S(2)}, u32[]{:S(2)}) collective-permute-start(f32[4,201,128]{2,1,0:T(8,128)S(1)} %get-tuple-element.6), channel_id=1, source_target_pairs={{0,480},{32,0},{64,32},{96,64},{128,96},{160,128},{192,160},{224,1... | collective-permute-start | bytes 1234952 | tf_op jit(solution)/shard_map/ppermute | solution.py:321

commit v5 on v4

--- a/solution.py
+++ b/solution.py
@@ -30,6 +30,16 @@
 
 def tile_index(i, j):
     return i * NT - i * (i - 1) // 2 + (j - i)
+
+
+def stacked_t(a, b):
+    left = jnp.concatenate(a, axis=0)
+    return dot_t(left, jnp.concatenate((b[0], b[0]), axis=0)) + dot_t(a[0], b[1])
+
+
+def stacked(a, b):
+    mm = functools.partial(jnp.dot, preferred_element_type=F32)
+    return mm(jnp.concatenate(a, axis=1), jnp.concatenate((b[0], b[0]), axis=0)) + mm(a[0], b[1])
 
 
 def packed_tiles():
@@ -181,7 +191,7 @@
 def update_after(p, s_ref, d_ref, inv_ref):
     base = p * T
     after = base + T
-    panel = dot3(halves(inv_ref[...]), halves(s_ref[base:after, base:]))
+    panel = stacked(halves(inv_ref[...]), halves(s_ref[base:after, base:]))
     upper = lax.broadcasted_iota(jnp.int32, (T, T), 1) >= lax.broadcasted_iota(jnp.int32, (T, T), 0)
     s_ref[base:after, base:after] = jnp.where(upper, panel[:, :T], 0.0)
     if after == COLS:
@@ -193,7 +203,7 @@
         lo = i * T - after
         left = tuple(v[:, lo : lo + T] for v in split)
         right = tuple(v[:, lo:] for v in split)
-        block = s_ref[i * T : (i + 1) * T, i * T :] - dot3_t(left, right)
+        block = s_ref[i * T : (i + 1) * T, i * T :] - stacked_t(left, right)
         s_ref[i * T : (i + 1) * T, i * T :] = block
         if i == p + 1:
             d_ref[...] = block[:, :T]

time: 152 us -> 151 us (level)
  no operation moved by 1% of the time
where the time goes in v5:
time: 151 us
  blocking collectives  98.2 us (65%)
  Pallas kernels  34.5 us (23%)
  starting transfers between devices  8.79 us (6%)
  waiting for transfers between devices  6 us (4%)
  local copies, waits for them, and re-layouts  1.92 us (1%)
    unnamed x1, blocking collectives  39.8 us
    all_gather x1, blocking collectives, shards(): own = lax.all_gather(piece, 'leaf', axis=0, axis_index_groups=groups)  29.6 us
    all_to_all x1, blocking collectives, shards(): got = lax.all_to_all(pay, 'front', 0, 0, tiled=True)  28.8 us
    pallas_call x1, Pallas kernels, factor(): pl.pallas_call(factor_kernel, out_shape=(jax.ShapeDtypeStruct((1, PIV //...  26 us
    pallas_call x1, Pallas kernels, local_gram(): pl.pallas_call(gram_kernel, out_shape=jax.ShapeDtypeStruct((NLEAF * SHARD...  7.23 us
    ppermute x1, waiting for transfers between devices, shards(): lax.ppermute(own[:HALF], 'leaf', [(z, (z + 1) % NLEAF) for z in range(NLE...  5.65 us
    ppermute x1, starting transfers between devices, shards(): lax.ppermute(own[HALF:], 'leaf', [(z, (z - 1) % NLEAF) for z in range(NLE...  4.57 us
  transfers between devices with their start and end apart: 3, of which 2 were waited for; matrix products, arithmetic and copies ran while one was open for 1% of the time, Pallas kernels for 0%

profile of v5, /device:TPU:1, one launch (start us, length us, event | category | flops | bytes accessed | tf_op | source)
XLA Modules:
  0.0 150.8 jit_solution(8580630956290376930)
XLA Ops:
  0.6 7.2 %local_gram.1 = f32[3216,128]{1,0:T(8,128)} custom-call(f32[1,1024,896]{2,1,0:T(8,128)} %x_ref.1), custom_call_target="tpu_custom_call" | custom-call | tf_op jit(solution)/shard_map/local_gram/pallas_call | solution.py:122
  7.9 39.8 %fusion = f32[208,128]{1,0:T(8,128)S(1)} fusion(f32[3216,128]{1,0:T(8,128)} %local_gram.1), kind=kCustom, calls=%all-reduce-scatter | all-reduce-scatter fusion | flops 425985 | bytes 1755136
  47.6 0.0 copy-start
  47.7 0.0 copy-start.1
  47.7 2.3 %collective-permute-start.2 = (f32[105,128]{1,0:T(8,128)S(1)}, f32[105,128]{1,0:T(8,128)S(1)}, u32[]{:S(2)}, u32[]{:S(2)}) collective-permute-start(f32[105,128]{1,0:T(8,128)S(1)} %slice.14), channel_id=1, source_target_pairs={{0,32},{32,64},{64,96},{96,128},{128,160},{160,192},{192,224},{224... | collective-permute-start | bytes 161288
  50.0 1.3 dynamic-slice.4
  51.9 0.0 collective-permute-done.2
  51.9 0.4 concatenate
  52.3 29.6 %all-gather.1.g_ref = f32[8,201,128]{2,1,0:T(8,128)S(1)} all-gather(f32[1,201,128]{2,1,0:T(8,128)S(1)} %bitcast.14), channel_id=2, replica_groups={{0,64,128,192,256,320,384,448},{32,96,160,224,288,352,416,480},{1,65,12..., dimensions={0}, use_global_device_ids=true | all-gather | bytes 926208 | tf_op jit(solution)/shard_map/all_gather | solution.py:329
  81.9 0.1 fusion.1
  82.0 1.9 %collective-permute-start = (f32[4,201,128]{2,1,0:T(8,128)S(1)}, f32[4,201,128]{2,1,0:T(8,128)S(1)}, u32[]{:S(2)}, u32[]{:S(2)}) collective-permute-start(f32[4,201,128]{2,1,0:T(8,128)S(1)} %get-tuple-element.7), channel_id=1, source_target_pairs={{0,32},{32,64},{64,96},{96,128},{128,160},{160,192},{192,224},{224... | collective-permute-start | bytes 1234952 | tf_op jit(solution)/shard_map/ppermute | solution.py:330
  83.9 4.6 %collective-permute-start.1 = (f32[4,201,128]{2,1,0:T(8,128)S(1)}, f32[4,201,128]{2,1,0:T(8,128)S(1)}, u32[]{:S(2)}, u32[]{:S(2)}) collective-permute-start(f32[4,201,128]{2,1,0:T(8,128)S(1)} %get-tuple-element.6), channel_id=1, source_target_pairs={{0,480},{32,0},{64,32},{96,64},{128,96},{160,128},{192,160},{224,1... | collective-permute-start | bytes 1234952 | tf_op jit(solution)/shard_map/ppermute | solution.py:331
  88.5 0.0 copy-done
  88.5 0.1 copy.7.owner_ref
  88.6 0.0 copy-done.1
  88.6 0.1 copy.8.dest_ref
  88.7 5.6 %collective-permute-done.low_ref = f32[4,201,128]{2,1,0:T(8,128)S(1)} collective-permute-done((f32[4,201,128]{2,1,0:T(8,128)S(1)}, f32[4,201,128]{2,1,0:T(8,128)S(1)}, u32[]{:S(2)}, u32[]{:S(2)}) %collective-permute-start) | collective-permute-done | bytes 411680 | tf_op jit(solution)/shard_map/ppermute | solution.py:330
  94.3 0.3 collective-permute-done.1.high_ref
  94.7 26.0 %factor.1 = (f32[1,16,896]{2,1,0:T(8,128)}, f32[512,128]{1,0:T(8,128)S(1)}) custom-call(f32[8,201,128]{2,1,0:T(8,128)S(1)} %all-gather.1.g_ref, f32[4,201,128]{2,1,0:T(8,128)S(1)} %collective-permute-done.low_ref, f32[4,201,128]{2,1,0:T(8,128)S(1)} %collective-permute-done.1.high_ref, s32[1,40]{1,0:T(1,128)S(1)} %bitcast.13, s32[40,1]{1,0:T(8,128)S(1)} %copy.7.owner_ref, ...), custom_call_target="tpu_custom_call" | custom-call | tf_op jit(solution)/shard_map/factor/pallas_call | solution.py:284
  120.6 28.8 %all_to_all.11 = f32[32,16,128]{2,1,0:T(8,128)S(1)} all-to-all(f32[32,16,128]{2,1,0:T(8,128)S(1)} %bitcast.11), channel_id=1, replica_groups=mesh['leaf'=16,'front'=32] {'front'}, dimensions={0} | all-to-all | bytes 524288 | tf_op jit(solution)/shard_map/all_to_all | solution.py:336
  149.5 1.3 assemble.1
  (2 shorter events, 0.0 us)
Async XLA Ops:
  47.6 40.8 %copy-start = (s32[1,40,1]{1,2,0:T(1,128)S(1)}, s32[1,40,1]{1,2,0:T(1,128)}, u32[]{:S(2)}) copy-start(s32[1,40,1]{1,2,0:T(1,128)} %param.4) | copy-start | bytes 484
  47.7 40.9 %copy-start.1 = (s32[1,40]{1,0:T(1,128)S(1)}, s32[1,40]{1,0:T(1,128)}, u32[]{:S(2)}) copy-start(s32[1,40]{1,0:T(1,128)} %param.5) | copy-start | bytes 484
  47.7 4.2 %collective-permute-start.2 = (f32[105,128]{1,0:T(8,128)S(1)}, f32[105,128]{1,0:T(8,128)S(1)}, u32[]{:S(2)}, u32[]{:S(2)}) collective-permute-start(f32[105,128]{1,0:T(8,128)S(1)} %slice.14), channel_id=1, source_target_pairs={{0,32},{32,64},{64,96},{96,128},{128,160},{160,192},{192,224},{224... | collective-permute-start | bytes 161288
  82.0 12.4 %collective-permute-start = (f32[4,201,128]{2,1,0:T(8,128)S(1)}, f32[4,201,128]{2,1,0:T(8,128)S(1)}, u32[]{:S(2)}, u32[]{:S(2)}) collective-permute-start(f32[4,201,128]{2,1,0:T(8,128)S(1)} %get-tuple-element.7), channel_id=1, source_target_pairs={{0,32},{32,64},{64,96},{96,128},{128,160},{160,192},{192,224},{224... | collective-permute-start | bytes 1234952 | tf_op jit(solution)/shard_map/ppermute | solution.py:330
  83.9 10.8 %collective-permute-start.1 = (f32[4,201,128]{2,1,0:T(8,128)S(1)}, f32[4,201,128]{2,1,0:T(8,128)S(1)}, u32[]{:S(2)}, u32[]{:S(2)}) collective-permute-start(f32[4,201,128]{2,1,0:T(8,128)S(1)} %get-tuple-element.6), channel_id=1, source_target_pairs={{0,480},{32,0},{64,32},{96,64},{128,96},{160,128},{192,160},{224,1... | collective-permute-start | bytes 1234952 | tf_op jit(solution)/shard_map/ppermute | solution.py:331
